TPU v7x, 32 devices: a whole 2x2x4 slice. The times are simulated.
32 devices in a mesh: groups: 2 (over x), tensor: 4 (over y, core), dp: 4 (over z).
Axes of the slice: x: 2, y: 2, z: 4, core: 2. Of those that a mesh axis runs over, the one named last changes fastest.
Arguments:
- hidden_in: bfloat16 [1024, 8192], P(('groups', 'dp'), 'tensor'), parts along dimension 0, may hold values from -6 to 6
- out_grad: bfloat16 [1024, 8192], P(('groups', 'dp'), 'tensor'), parts along dimension 0, may hold values from -6 to 6
- w_gate_up: bfloat16 [2, 28672, 8192], P(None, ('tensor', 'dp')), may hold values from -0.0625 to 0.0625
- w_down: bfloat16 [28672, 8192], P(('tensor', 'dp')), may hold values from -0.03125 to 0.03125
- feat_proj: bfloat16 [8192, 192], P('tensor'), may hold values from -0.0625 to 0.0625
- unit_proj: bfloat16 [28672, 192], P(('tensor', 'dp')), may hold values from -0.03125 to 0.03125
- precond: float32 [3, 4096, 4096], P(None, ('tensor', 'dp')), may hold values from -20 to 20
Outputs:
- precond_grad: float32 [3, 8, 4096], P(None, 'groups', ('tensor', 'dp')), parts along dimension 1
There are 2 independent parts, one for each index of `groups`. A program takes and returns all parts, laid end to end along the dimension named above; an argument that names none is the same for every part. Nothing has to cross between parts.
All inputs are finite; a program needn't handle non-finite values.
Results may differ from a plain program's by a relative error of at most 0.0029.
Values may be sent and summed in bfloat16 or wider, within the bound.
No kernel may reach another device: no remote copies, remote signals or barrier semaphores. Data moves between devices by JAX's collectives and lax.ppermute only.
A program may use at most 256 MiB of HBM per device.

v0:
```python
import jax
import jax.numpy as jnp
from jax import lax
from jax.sharding import PartitionSpec as P

K = 64
SEQ = 128
contract_last = (((1,), (1,)), ((), ()))


def project_pair(rows_in, rows_out, columns):
    return jnp.concatenate(
        [
            jnp.dot(rows_in, columns[:, : 2 * K], preferred_element_type=jnp.float32),
            jnp.dot(rows_out, columns[:, 2 * K :], preferred_element_type=jnp.float32),
        ],
        axis=1,
    )


def form_sketch(in_side, out_side):
    seq_count = in_side.shape[0] // SEQ
    left_rows = in_side.reshape(seq_count, SEQ, 3, K)
    right_rows = out_side.reshape(seq_count, SEQ, 3, K)
    sketch = jnp.einsum("stwi,stwj->wsij", left_rows, right_rows, precision=lax.Precision.HIGHEST)
    sketch = sketch * SEQ ** (-0.5)
    return sketch.reshape(3, seq_count, K * K)


def local(hidden_in, out_grad, w_gate_up, w_down, feat_proj, unit_proj, precond):
    unit_width = w_down.shape[0]
    model_width = w_down.shape[1]
    w_both = w_gate_up.reshape(2 * unit_width, model_width)
    paired = jnp.stack([hidden_in, out_grad])
    tokens = hidden_in.shape[0] * lax.axis_size("dp")
    columns = lax.all_gather(feat_proj, "tensor", axis=0, tiled=True)
    feat_side = None
    rows_all = lax.all_gather(paired, "dp", axis=1, tiled=True)
    initial = [
        jnp.zeros((tokens, 2 * unit_width), jnp.float32),
        jnp.zeros((tokens, unit_width), jnp.float32),
    ]
    initial.append(jnp.zeros((tokens, 3 * K), jnp.float32))
    pieces = lax.all_gather(rows_all, "tensor", axis=2, tiled=True)
    result = [
        lax.dot_general(pieces[0], w_both, contract_last, preferred_element_type=jnp.float32),
        lax.dot_general(pieces[1], w_down, contract_last, preferred_element_type=jnp.float32),
    ]
    result.append(project_pair(pieces[0], pieces[1], columns))
    folded = tuple(result)
    pre_act = folded[0]
    hid_grad = folded[1]
    feat_side = folded[2]
    gate_pre = pre_act[:, :unit_width]
    up_pre = pre_act[:, unit_width:]
    gate_sig = jax.nn.sigmoid(gate_pre)
    silu_gate = gate_pre * gate_sig
    hidden = (silu_gate * up_pre).astype(jnp.bfloat16)
    gate_grad = (hid_grad * up_pre * gate_sig * (1.0 + gate_pre * (1.0 - gate_sig))).astype(
        jnp.bfloat16
    )
    up_grad = (hid_grad * silu_gate).astype(jnp.bfloat16)
    unit_part = jnp.concatenate(
        [
            jnp.dot(gate_grad, unit_proj[:, :K], preferred_element_type=jnp.float32),
            jnp.dot(up_grad, unit_proj[:, K : 2 * K], preferred_element_type=jnp.float32),
            jnp.dot(hidden, unit_proj[:, 2 * K :], preferred_element_type=jnp.float32),
        ],
        axis=1,
    )
    unit_side = lax.psum(unit_part, ("tensor", "dp"))
    in_side = jnp.concatenate([feat_side[:, : 2 * K], unit_side[:, 2 * K :]], axis=1)
    out_side = jnp.concatenate([unit_side[:, : 2 * K], feat_side[:, 2 * K :]], axis=1)
    sketch = form_sketch(in_side, out_side)
    return jnp.einsum("wrc,wsc->wsr", precond, sketch, precision=lax.Precision.HIGHEST)


def solution(mesh):
    in_specs = (
        P(("groups", "dp"), "tensor"),
        P(("groups", "dp"), "tensor"),
        P(None, ("tensor", "dp"), None),
        P(("tensor", "dp"), None),
        P("tensor", None),
        P(("tensor", "dp"), None),
        P(None, ("tensor", "dp"), None),
    )
    out_specs = P(None, "groups", ("tensor", "dp"))
    return jax.shard_map(local, mesh=mesh, in_specs=in_specs, out_specs=out_specs, check_vma=False)
```

profile of v0, /device:TPU:0, one launch (start us, length us, event | category | flops | bytes accessed | tf_op | source)
XLA Modules:
  0.0 386.8 jit_solution(336281864798562320)
XLA Ops:
  6.5 0.0 all-gather.4.cloned.1.call-start
  6.5 2.3 pad_maximum_fusion
  8.8 0.0 all-gather.4.cloned.1.call-update
  8.8 0.0 all-gather.6.cloned.1.call-start
  8.9 83.6 %all-gather.4.cloned.1.call-done = bf16[2,512,2048]{2,1,0:T(8,128)(2,1)} async-done(((bf16[2,128,2048]{2,1,0:T(8,128)(2,1)}), bf16[2,512,2048]{2,1,0:T(8,128)(2,1)}) %all-gather.4.cloned.1.call-update) | async-done | bytes 4194320 | tf_op jit(solution)/shard_map/all_gather | solution.py:38
  92.4 0.0 all-gather.6.cloned.1.call-update
  92.5 0.0 all-gather.8.cloned.1.call-start
  92.5 0.7 all-gather.8.cloned.1.call-update
  93.2 0.0 all-reduce.2.cloned.1.call-start
  93.3 105.2 %all-gather.6.cloned.1.call-done = bf16[2,512,8192]{2,1,0:T(8,128)(2,1)} async-done(((bf16[2,512,2048]{2,1,0:T(8,128)(2,1)}), bf16[2,512,8192]{2,1,0:T(8,128)(2,1)}) %all-gather.6.cloned.1.call-update) | async-done | bytes 16777232 | tf_op jit(solution)/shard_map/all_gather | solution.py:44
  198.5 0.0 copy-start
  198.5 38.6 %fusion = f32[512,3584]{1,0:T(8,128)} fusion(bf16[3584,8192]{1,0:T(8,128)(2,1)} %bitcast.23, bf16[2,512,8192]{2,1,0:T(8,128)(2,1)} %all-gather.6.cloned.1.call-done), kind=kOutput, calls=%fused_computation.2 | convolution fusion | flops 30064771072 | bytes 74448896 | tf_op jit(solution)/shard_map/dot_general | solution.py:46
  237.1 0.0 copy-done
  237.1 4.3 %fusion.7 = f32[512,64]{0,1:T(8,128)S(1)} fusion(f32[512,3584]{1,0:T(8,128)} %fusion, bf16[1792,192]{0,1:T(8,128)(2,1)S(1)} %copy-done), kind=kOutput, calls=%fused_computation.13 | convolution fusion | flops 122945536 | bytes 7700480 | tf_op jit(solution)/shard_map/dot_general | solution.py:67
  241.3 22.9 %fusion.3 = f32[512,1792]{1,0:T(8,128)} fusion(bf16[1792,8192]{1,0:T(8,128)(2,1)} %param.10, bf16[2,512,8192]{2,1,0:T(8,128)(2,1)} %all-gather.6.cloned.1.call-done), kind=kOutput, calls=%fused_computation.5 | convolution fusion | flops 15032385536 | bytes 41418752 | tf_op jit(solution)/shard_map/dot_general | solution.py:47
  264.3 0.0 copy-start.1
  264.3 0.0 copy-start.2
  264.3 4.4 %fusion.6 = f32[512,64]{0,1:T(8,128)S(1)} fusion(f32[512,1792]{1,0:T(8,128)} %fusion.3, f32[512,3584]{1,0:T(8,128)} %fusion, bf16[1792,192]{0,1:T(8,128)(2,1)S(1)} %copy-done), kind=kOutput, calls=%fused_computation.12 | convolution fusion | flops 122945536 | bytes 7700480 | tf_op jit(solution)/shard_map/dot_general | solution.py:66
  268.7 0.8 copy-done.1
  269.5 1.0 copy-done.2
  270.5 1.6 fusion.8
  272.1 0.8 pad_maximum_fusion.1
  272.9 0.0 all-reduce.2.cloned.1.call-update
  272.9 0.0 all-gather.8.cloned.1.call-done
  272.9 6.9 %fusion.1 = f32[512,128]{0,1:T(8,128)S(1)} fusion(bf16[2,512,8192]{2,1,0:T(8,128)(2,1)} %all-gather.6.cloned.1.call-done, bf16[8192,192]{0,1:T(8,128)(2,1)} %all-gather.8.cloned.1.call-done), kind=kOutput, calls=%fused_computation.3 | convolution fusion | flops 1073741824 | bytes 10747904 | tf_op jit(solution)/shard_map/dot_general | solution.py:14
  279.8 6.3 %fusion.2 = f32[512,64]{0,1:T(8,128)S(1)} fusion(bf16[2,512,8192]{2,1,0:T(8,128)(2,1)} %all-gather.6.cloned.1.call-done, bf16[8192,192]{0,1:T(8,128)(2,1)} %all-gather.8.cloned.1.call-done), kind=kOutput, calls=%fused_computation.4 | convolution fusion | flops 536870912 | bytes 9568256 | tf_op jit(solution)/shard_map/dot_general | solution.py:15
  286.1 77.3 %all-reduce.2.cloned.1.call-done = f32[512,192]{0,1:T(8,128)} async-done(((f32[512,192]{0,1:T(8,128)}), f32[512,192]{0,1:T(8,128)}) %all-reduce.2.cloned.1.call-update) | async-done | bytes 393232 | tf_op jit(solution)/shard_map/psum | solution.py:71
  363.4 0.9 slice.51
  364.4 0.1 reshape.13
  364.5 1.0 slice.52
  365.5 0.1 reshape.14
  365.7 0.8 convolution_multiply_fusion
  366.4 0.2 reshape.15
  366.6 13.6 %fusion.20 = f32[3,4,256]{2,1,0:T(4,128)} fusion(f32[3,4,4096]{2,1,0:T(4,128)S(1)} %reshape.15, f32[3,256,4096]{2,1,0:T(8,128)} %param.13), kind=kOutput, calls=%fused_computation.29 | convolution fusion | flops 150994944 | bytes 12791808 | tf_op jit(solution)/shard_map/wrc,wsc->wsr/dot_general | solution.py:75
  (2 shorter events, 0.1 us)
Async XLA Ops:
  6.5 85.9 %all-gather.4.cloned.1.call-start = ((), (), s32[]{:S(2)}) async-start(), calls=%async_computation | async-start | bytes 5242880 | tf_op jit(solution)/shard_map/all_gather | solution.py:38
  8.8 189.7 %all-gather.6.cloned.1.call-start = ((), (), s32[]{:S(2)}) async-start(), calls=%async_computation.1 | async-start | bytes 20971520 | tf_op jit(solution)/shard_map/all_gather | solution.py:44
  92.5 180.4 %all-gather.8.cloned.1.call-start = ((), (), s32[]{:S(2)}) async-start(), calls=%async_computation.2 | async-start | bytes 3932160 | tf_op jit(solution)/shard_map/all_gather | solution.py:36
  93.2 270.2 %all-reduce.2.cloned.1.call-start = ((), (), s32[]{:S(2)}) async-start(), calls=%async_computation.3 | async-start | bytes 786432 | tf_op jit(solution)/shard_map/psum | solution.py:71
  198.5 38.6 %copy-start = (bf16[1792,192]{0,1:T(8,128)(2,1)S(1)}, bf16[1792,192]{0,1:T(8,128)(2,1)}, u32[]{:S(2)}) copy-start(bf16[1792,192]{0,1:T(8,128)(2,1)} %param.12) | copy-start | bytes 2064388
  264.3 5.2 %copy-start.1 = (f32[512,3584]{1,0:T(8,128)S(1)}, f32[512,3584]{1,0:T(8,128)}, u32[]{:S(2)}) copy-start(f32[512,3584]{1,0:T(8,128)} %fusion) | copy-start | bytes 22020100
  264.3 6.3 %copy-start.2 = (f32[512,1792]{1,0:T(8,128)S(1)}, f32[512,1792]{1,0:T(8,128)}, u32[]{:S(2)}) copy-start(f32[512,1792]{1,0:T(8,128)} %fusion.3) | copy-start | bytes 11010052
Sparse Core Ops, SparseCore 0:
  9.0 83.4 all-gather.3
  94.0 104.4 all-gather.5
  200.1 28.5 all-gather.7
  273.0 90.3 all-reduce.1
where the time goes:
time: 387 us
  waiting for transfers between devices  267 us (69%)
  matrix products  99.3 us (26%)
  between operations  13.2 us (3%)
  local copies, waits for them, and re-layouts  4.2 us (1%)
    all_gather x1, waiting for transfers between devices, local(): pieces = lax.all_gather(rows_all, 'tensor', axis=2, tiled=True)  105 us
    all_gather x1, waiting for transfers between devices, local(): rows_all = lax.all_gather(paired, 'dp', axis=1, tiled=True)  83.6 us
    psum x1, waiting for transfers between devices, local(): unit_side = lax.psum(unit_part, ('tensor', 'dp'))  77.3 us
    dot_general x1, matrix products, local(): lax.dot_general(pieces[0], w_both, contract_last, preferred_element_type=...  38.6 us
    dot_general x1, matrix products, local(): lax.dot_general(pieces[1], w_down, contract_last, preferred_element_type=...  22.9 us
    dot_general x1, matrix products, local(): jnp.einsum('wrc,wsc->wsr', precond, sketch, precision=lax.Precision.HIGHEST)  13.6 us
  transfers between devices with their start and end apart: 4, of which 3 were waited for; matrix products, arithmetic and copies ran while one was open for 22% of the time, Pallas kernels for 0%

commit v1 on v0

--- a/solution.py
+++ b/solution.py
@@ -6,6 +6,11 @@
 K = 64
 SEQ = 128
 contract_last = (((1,), (1,)), ((), ()))
+
+
+def raise_panel_now(m):
+    long_array = jnp.sum(jax.lax.all_gather(m, axis_name=("tensor", "dp")), axis=0)
+    return long_array
 
 
 def project_pair(rows_in, rows_out, columns):
@@ -68,7 +73,7 @@
         ],
         axis=1,
     )
-    unit_side = lax.psum(unit_part, ("tensor", "dp"))
+    unit_side = raise_panel_now(unit_part)
     in_side = jnp.concatenate([feat_side[:, : 2 * K], unit_side[:, 2 * K :]], axis=1)
     out_side = jnp.concatenate([unit_side[:, : 2 * K], feat_side[:, 2 * K :]], axis=1)
     sketch = form_sketch(in_side, out_side)

time: 387 us -> 367 us (0.948)
  waiting for transfers between devices: 267 us -> 239 us
  local copies, waits for them, and re-layouts: 4.2 us -> 10.8 us
    psum x1 -> x0, waiting for transfers between devices: 77.3 us -> none  [local(): unit_side = lax.psum(unit_part, ('tensor', 'dp'))]
    all_gather x0 -> x1, waiting for transfers between devices: none -> 49 us  [raise_panel_now(): jax.lax.all_gather(m, axis_name=('tensor', 'dp'))]
    unnamed x6 -> x9, local copies, waits for them, and re-layouts: 1.86 us -> 10.3 us
  transfers between devices with their start and end apart: 4 -> 4, of which waited for: 3 -> 3; matrix products, arithmetic and copies ran while one was open for 22% -> 23% of each run, Pallas kernels for 0% -> 0%
where the time goes in v1:
time: 367 us; the launch traced here: 366 us
  waiting for transfers between devices  239 us (65%)
  matrix products  99.2 us (27%)
  between operations  13.2 us (4%)
  local copies, waits for them, and re-layouts  10.8 us (3%)
  other arithmetic  4.54 us (1%)
    all_gather x1, waiting for transfers between devices, local(): pieces = lax.all_gather(rows_all, 'tensor', axis=2, tiled=True)  105 us
    all_gather x1, waiting for transfers between devices, local(): rows_all = lax.all_gather(paired, 'dp', axis=1, tiled=True)  83.6 us
    all_gather x1, waiting for transfers between devices, raise_panel_now(): jax.lax.all_gather(m, axis_name=('tensor', 'dp'))  49 us
    dot_general x1, matrix products, local(): lax.dot_general(pieces[0], w_both, contract_last, preferred_element_type=...  38.6 us
    dot_general x1, matrix products, local(): lax.dot_general(pieces[1], w_down, contract_last, preferred_element_type=...  22.9 us
    dot_general x1, matrix products, local(): jnp.einsum('wrc,wsc->wsr', precond, sketch, precision=lax.Precision.HIGHEST)  13.6 us
    unnamed x9, local copies, waits for them, and re-layouts  10.3 us
  transfers between devices with their start and end apart: 4, of which 3 were waited for; matrix products, arithmetic and copies ran while one was open for 23% of the time, Pallas kernels for 0%

profile of v1, /device:TPU:0, one launch (start us, length us, event | category | flops | bytes accessed | tf_op | source)
XLA Modules:
  0.0 366.3 jit_solution(184224654995826279)
XLA Ops:
  6.5 0.0 all-gather.6.cloned.1.call-start
  6.5 2.3 pad_maximum_fusion
  8.8 0.0 all-gather.6.cloned.1.call-update
  8.8 0.0 all-gather.8.cloned.1.call-start
  8.9 83.6 %all-gather.6.cloned.1.call-done = bf16[2,512,2048]{2,1,0:T(8,128)(2,1)} async-done(((bf16[2,128,2048]{2,1,0:T(8,128)(2,1)}), bf16[2,512,2048]{2,1,0:T(8,128)(2,1)}) %all-gather.6.cloned.1.call-update) | async-done | bytes 4194320 | tf_op jit(solution)/shard_map/all_gather | solution.py:43
  92.4 0.0 all-gather.8.cloned.1.call-update
  92.5 0.0 all-gather.10.cloned.1.call-start
  92.5 0.7 all-gather.10.cloned.1.call-update
  93.2 0.0 all-gather.12.cloned.1.call-start
  93.3 105.2 %all-gather.8.cloned.1.call-done = bf16[2,512,8192]{2,1,0:T(8,128)(2,1)} async-done(((bf16[2,512,2048]{2,1,0:T(8,128)(2,1)}), bf16[2,512,8192]{2,1,0:T(8,128)(2,1)}) %all-gather.8.cloned.1.call-update) | async-done | bytes 16777232 | tf_op jit(solution)/shard_map/all_gather | solution.py:49
  198.5 0.0 copy-start.1
  198.5 38.6 %fusion = f32[512,3584]{1,0:T(8,128)} fusion(bf16[3584,8192]{1,0:T(8,128)(2,1)} %bitcast.29, bf16[2,512,8192]{2,1,0:T(8,128)(2,1)} %all-gather.8.cloned.1.call-done), kind=kOutput, calls=%fused_computation.2 | convolution fusion | flops 30064771072 | bytes 74448896 | tf_op jit(solution)/shard_map/dot_general | solution.py:51
  237.1 0.0 copy-done.1
  237.1 4.3 %fusion.7 = f32[512,64]{0,1:T(8,128)S(1)} fusion(f32[512,3584]{1,0:T(8,128)} %fusion, bf16[1792,192]{0,1:T(8,128)(2,1)S(1)} %copy-done.1), kind=kOutput, calls=%fused_computation.14 | convolution fusion | flops 122945536 | bytes 7700480 | tf_op jit(solution)/shard_map/dot_general | solution.py:72
  241.3 22.9 %fusion.3 = f32[512,1792]{1,0:T(8,128)} fusion(bf16[1792,8192]{1,0:T(8,128)(2,1)} %param.10, bf16[2,512,8192]{2,1,0:T(8,128)(2,1)} %all-gather.8.cloned.1.call-done), kind=kOutput, calls=%fused_computation.5 | convolution fusion | flops 15032385536 | bytes 41418752 | tf_op jit(solution)/shard_map/dot_general | solution.py:52
  264.2 0.0 copy-start.2
  264.2 0.0 copy-start.3
  264.2 4.4 %fusion.6 = f32[512,64]{0,1:T(8,128)S(1)} fusion(f32[512,1792]{1,0:T(8,128)} %fusion.3, f32[512,3584]{1,0:T(8,128)} %fusion, bf16[1792,192]{0,1:T(8,128)(2,1)S(1)} %copy-done.1), kind=kOutput, calls=%fused_computation.13 | convolution fusion | flops 122945536 | bytes 7700480 | tf_op jit(solution)/shard_map/dot_general | solution.py:71
  268.6 0.8 copy-done.2
  269.5 1.0 copy-done.3
  270.5 1.6 fusion.8
  272.1 0.8 pad_maximum_fusion.1
  272.9 0.0 all-gather.12.cloned.1.call-update
  272.9 0.0 all-gather.10.cloned.1.call-done
  272.9 0.0 copy-start
  272.9 6.4 %fusion.2 = f32[512,64]{0,1:T(8,128)S(1)} fusion(bf16[2,512,8192]{2,1,0:T(8,128)(2,1)} %all-gather.8.cloned.1.call-done, bf16[8192,192]{0,1:T(8,128)(2,1)} %all-gather.10.cloned.1.call-done), kind=kOutput, calls=%fused_computation.4 | convolution fusion | flops 536870912 | bytes 9568256 | tf_op jit(solution)/shard_map/dot_general | solution.py:20
  279.3 0.0 copy-done
  279.3 6.7 %fusion.1 = f32[512,128]{0,1:T(8,128)S(1)} fusion(bf16[2,512,8192]{2,1,0:T(8,128)(2,1)} %all-gather.8.cloned.1.call-done, bf16[8192,192]{0,1:T(8,128)(2,1)S(1)} %copy-done), kind=kOutput, calls=%fused_computation.3 | convolution fusion | flops 1073741824 | bytes 10747904 | tf_op jit(solution)/shard_map/dot_general | solution.py:19
  286.0 49.0 %all-gather.12.cloned.1.call-done = f32[8192,192]{0,1:T(8,128)} async-done(((f32[512,192]{0,1:T(8,128)}), f32[8192,192]{0,1:T(8,128)}) %all-gather.12.cloned.1.call-update) | async-done | bytes 6291472 | tf_op jit(solution)/shard_map/all_gather | solution.py:12
  335.0 8.4 %copy.10 = f32[24,8,16,512]{3,2,1,0:T(8,128)S(1)} copy(f32[24,8,16,512]{3,1,2,0:T(8,128)} %bitcast.26) | data formatting | bytes 12582912
  343.4 1.4 bitcast_reduce_fusion
  344.9 0.1 reshape.14
  345.1 0.1 reshape.13
  345.2 0.8 convolution_multiply_fusion
  346.0 0.2 reshape.15
  346.2 13.6 %fusion.20 = f32[3,4,256]{2,1,0:T(4,128)} fusion(f32[3,4,4096]{2,1,0:T(4,128)S(1)} %reshape.15, f32[3,256,4096]{2,1,0:T(8,128)} %param.13), kind=kOutput, calls=%fused_computation.30 | convolution fusion | flops 150994944 | bytes 12791808 | tf_op jit(solution)/shard_map/wrc,wsc->wsr/dot_general | solution.py:80
  (4 shorter events, 0.1 us)
Async XLA Ops:
  6.5 85.9 %all-gather.6.cloned.1.call-start = ((), (), s32[]{:S(2)}) async-start(), calls=%async_computation | async-start | bytes 5242880 | tf_op jit(solution)/shard_map/all_gather | solution.py:43
  8.8 189.7 %all-gather.8.cloned.1.call-start = ((), (), s32[]{:S(2)}) async-start(), calls=%async_computation.1 | async-start | bytes 20971520 | tf_op jit(solution)/shard_map/all_gather | solution.py:49
  92.5 180.4 %all-gather.10.cloned.1.call-start = ((), (), s32[]{:S(2)}) async-start(), calls=%async_computation.2 | async-start | bytes 3932160 | tf_op jit(solution)/shard_map/all_gather | solution.py:41
  93.2 241.8 %all-gather.12.cloned.1.call-start = ((), (), s32[]{:S(2)}) async-start(), calls=%async_computation.3 | async-start | bytes 6684672 | tf_op jit(solution)/shard_map/all_gather | solution.py:12
  198.5 38.6 %copy-start.1 = (bf16[1792,192]{0,1:T(8,128)(2,1)S(1)}, bf16[1792,192]{0,1:T(8,128)(2,1)}, u32[]{:S(2)}) copy-start(bf16[1792,192]{0,1:T(8,128)(2,1)} %param.12) | copy-start | bytes 2064388
  264.2 5.2 %copy-start.2 = (f32[512,3584]{1,0:T(8,128)S(1)}, f32[512,3584]{1,0:T(8,128)}, u32[]{:S(2)}) copy-start(f32[512,3584]{1,0:T(8,128)} %fusion) | copy-start | bytes 22020100
  264.2 6.3 %copy-start.3 = (f32[512,1792]{1,0:T(8,128)S(1)}, f32[512,1792]{1,0:T(8,128)}, u32[]{:S(2)}) copy-start(f32[512,1792]{1,0:T(8,128)} %fusion.3) | copy-start | bytes 11010052
  272.9 6.4 %copy-start = (bf16[8192,192]{0,1:T(8,128)(2,1)S(1)}, bf16[8192,192]{0,1:T(8,128)(2,1)}, u32[]{:S(2)}) copy-start(bf16[8192,192]{0,1:T(8,128)(2,1)} %all-gather.10.cloned.1.call-done) | copy-start | bytes 9437188
Sparse Core Ops, SparseCore 0:
  8.9 83.4 all-gather.5
  94.0 104.4 all-gather.7
  200.1 28.5 all-gather.9
  273.0 61.9 all-gather.11
